TPU v7x, 256 devices: a whole 4x4x8 slice. The times are simulated.
256 devices in a mesh: dp: 64 (over z_hi, x, y, core), slab: 4 (over z_lo).
Axes of the slice: x: 4, y: 4, z: 8 (z_hi: 2, z_lo: 4; z = z_hi * 4 + z_lo), core: 2. Of those that a mesh axis runs over, the one named last changes fastest.
Arguments:
- images: bfloat16 [64, 256, 32, 128], P('dp', 'slab'), may hold values from -6 to 6
- cotangent: bfloat16 [64, 128, 64, 256], P('dp', None, 'slab'), may hold values from -6 to 6
- kernel: bfloat16 [3, 3, 256, 128], replicated, may hold values from -0.125 to 0.125
Outputs:
- grad_images: bfloat16 [64, 256, 32, 128], P('dp', 'slab')
- grad_kernel: float32 [3, 3, 256, 128], replicated
All inputs are finite; a program needn't handle non-finite values.
Results may differ from a plain program's by a relative error of at most 0.0034.
Values may be sent and summed in bfloat16 or wider, within the bound.
No kernel may reach another device: no remote copies, remote signals or barrier semaphores. Data moves between devices by JAX's collectives and lax.ppermute only.
A program may use at most 64 MiB of HBM per device.

v0:
```python
import jax
import jax.numpy as jnp
from jax import lax
from jax.sharding import PartitionSpec as P


def extended(cells, sides, width):
    for axis, dim in sides:
        count = lax.axis_size(axis)
        ends = count - 1
        head = lax.slice_in_dim(cells, 0, width, axis=dim)
        tail = lax.slice_in_dim(cells, cells.shape[dim] - width, cells.shape[dim], axis=dim)
        cells = jnp.concatenate(
            [
                lax.ppermute(tail, axis, [(i, (i + 1) % count) for i in range(ends)]),
                cells,
                lax.ppermute(head, axis, [((i + 1) % count, i) for i in range(ends)]),
            ],
            axis=dim,
        )
    return cells


def upsample(field):
    return jnp.repeat(jnp.repeat(field, 2, axis=2), 2, axis=3)


def downsum(field):
    count, chans, rows, cols = field.shape
    return field.reshape(count, chans, rows // 2, 2, cols // 2, 2).sum(axis=(3, 5))


def kernel_terms(padded_up, grad_rows):
    return lax.conv_general_dilated(
        padded_up,
        grad_rows,
        (1, 1),
        ((0, 0), (1, 1)),
        dimension_numbers=("CNHW", "IOHW", "HWNC"),
        preferred_element_type=jnp.float32,
    )


def input_terms(padded_grad, kernel):
    flipped = kernel[::-1, ::-1]
    return lax.conv_general_dilated(
        padded_grad,
        flipped,
        (1, 1),
        ((0, 0), (1, 1)),
        dimension_numbers=("NCHW", "HWOI", "NCHW"),
        preferred_element_type=jnp.float32,
    )


def body(images, cotangent, kernel):
    slab_up = lax.all_to_all(upsample(images), "slab", split_axis=2, concat_axis=1, tiled=True)
    padded_up = extended(slab_up, (("slab", 2),), 1)
    padded_grad = extended(cotangent, (("slab", 2),), 1)
    partial_kernel = kernel_terms(padded_up, cotangent)
    grad_low = downsum(input_terms(padded_grad, kernel))
    returned = lax.all_to_all(
        grad_low.astype(jnp.bfloat16), "slab", split_axis=1, concat_axis=2, tiled=True
    ).astype(grad_low.dtype)
    total = lax.psum(partial_kernel, ("dp", "slab"))
    return (returned.astype(jnp.bfloat16), total)


def solution(mesh):
    placed = (P("dp", "slab", None, None), P("dp", None, "slab", None), P())
    return jax.shard_map(
        body,
        mesh=mesh,
        in_specs=placed,
        out_specs=(P("dp", "slab", None, None), P()),
        check_vma=False,
    )
```

profile of v0, /device:TPU:6, one launch (start us, length us, event | category | flops | bytes accessed | tf_op | source)
XLA Modules:
  0.0 440.7 jit_solution(2120381636830538440)
XLA Ops:
  7.2 0.0 copy-start
  7.2 1.3 copy.36
  8.5 1.3 broadcast_in_dim.10
  9.8 4.7 %copy.37 = bf16[64,64,128]{1,0,2:T(8,128)(2,1)S(1)} copy(bf16[64,64,128]{2,0,1:T(8,128)(2,1)} %bitcast.38) | data formatting | bytes 2097152 | tf_op jit(solution)/shard_map/broadcast_in_dim | solution.py:25
  14.5 3.3 broadcast_in_dim.12
  17.8 7.8 %copy.38 = bf16[1,64,64,256]{3,1,0,2:T(8,128)(2,1)} copy(bf16[1,64,64,256]{2,1,3,0:T(8,128)(2,1)} %bitcast.35) | data formatting | bytes 4194304 | tf_op jit(solution)/shard_map/broadcast_in_dim | solution.py:25
  25.6 5.9 %all-to-all-start.1 = ((bf16[1,64,64,256]{3,1,0,2:T(8,128)(2,1)}), bf16[1,64,64,256]{3,1,0,2:T(8,128)(2,1)S(1)}, u32[]{:S(2)}, u32[]{:S(2)}) async-start(bf16[1,64,64,256]{3,1,0,2:T(8,128)(2,1)} %copy.38), calls=%async_computation.1 | async-start | bytes 4194304 | tf_op jit(solution)/shard_map/all_to_all | solution.py:57
  31.5 1.4 fusion.14
  32.9 3.9 collective-permute-start
  36.8 1.5 collective-permute-start.1
  38.3 4.5 %copy.44 = bf16[1,128,16,256]{1,0,3,2:T(2,128)(2,1)} copy(bf16[1,128,16,256]{3,2,1,0:T(8,128)(2,1)} %param.4) | data formatting | bytes 2097152 | tf_op args[1]
  42.8 25.4 %collective-permute-done = bf16[1,128,1,256]{3,2,1,0:T(2,128)(2,1)S(1)} collective-permute-done((bf16[1,128,1,256]{3,2,1,0:T(2,128)(2,1)S(1)}, bf16[1,128,1,256]{3,2,1,0:T(2,128)(2,1)S(1)}, u32[]{:S(2)}, u32[]{:S(2)}) %collective-permute-start) | collective-permute-done | bytes 65568 | tf_op jit(solution)/shard_map/ppermute | solution.py:15
  68.2 0.0 collective-permute-done.1
  68.2 3.4 maximum_bitcast_fusion
  71.6 2.7 copy.45
  74.3 2.6 pad.clone
  76.9 0.0 copy-start.2
  76.9 3.0 reshape.29
  79.9 1.5 copy.32
  81.5 0.0 copy-done
  81.5 0.0 copy-done.2
  81.5 3.0 broadcast_select_fusion
  84.5 3.3 copy.33
  87.9 0.0 all-to-all-done.1
  87.9 1.2 copy.39
  89.0 0.2 copy.40
  89.2 5.1 %copy.41 = bf16[1,256,16,256]{1,0,3,2:T(2,128)(2,1)} copy(bf16[1,256,16,256]{3,2,1,0:T(8,128)(2,1)S(1)} %bitcast.36) | data formatting | bytes 4194304 | tf_op jit(solution)/shard_map/all_to_all | solution.py:57
  94.3 2.3 fusion.13
  96.6 17.5 %collective-permute-start.2 = (bf16[1,256,1,256]{1,0,3,2:T(2,128)(2,1)}, bf16[1,256,1,256]{1,0,3,2:T(2,128)(2,1)}, u32[]{:S(2)}, u32[]{:S(2)}) collective-permute-start(bf16[1,256,1,256]{1,0,3,2:T(2,128)(2,1)} %get-tuple-element.2), channel_id=1, source_target_pairs={{0,1},{1,2},{2,3},{4,5},{5,6},{6,7},{8,9},{9,10},{10,11},{12,13},{... | collective-permute-start | bytes 393224 | tf_op jit(solution)/shard_map/ppermute | solution.py:15
  114.1 1.5 collective-permute-start.3
  115.6 4.6 %slice_bitcast_fusion = f32[1,256,16,256]{1,2,3,0:T(8,128)} fusion(f32[16,1,264,256]{3,0,2,1:T(8,128)} %bitcast.34), kind=kLoop, calls=%fused_computation.2 | loop fusion | bytes 8388608 | tf_op jit(solution)/shard_map/conv_general_dilated | solution.py:46
  120.2 5.8 %reshape.26 = f32[256,8,2,128,2]{0,2,1,4,3:T(2,128)} reshape(f32[1,256,16,256]{1,2,3,0:T(8,128)} %slice_bitcast_fusion) | data formatting | bytes 8388608 | tf_op jit(solution)/shard_map/reshape | solution.py:30
  126.0 0.0 copy-start.1
  126.0 5.9 %reduce_sum.9 = bf16[256,8,128]{0,1,2:T(8,128)(2,1)S(1)} reduce(f32[256,8,2,128,2]{0,2,1,4,3:T(2,128)} %reshape.26, f32[]{:T(128)} %constant.0.clone.1), dimensions={2,4}, to_apply=%region_0.0 | reduce | flops 786432 | bytes 4718596 | tf_op jit(solution)/shard_map/reduce_sum | solution.py:30
  131.9 1.3 copy.34
  133.2 4.2 all-to-all-start
  137.4 0.0 all-reduce.2.cloned.1.call-start
  137.4 0.0 collective-permute-done.2
  137.4 0.0 collective-permute-done.3
  137.5 0.0 copy-done.1
  137.5 30.8 %fusion = f32[3,3,256,128]{3,2,1,0:T(8,128)} fusion(bf16[1,128,16,256]{1,0,3,2:T(2,128)(2,1)S(1)} %copy-done.1, bf16[1,256,1,256]{1,0,3,2:T(2,128)(2,1)} %collective-permute-done.3, bf16[1,256,16,256]{1,0,3,2:T(2,128)(2,1)} %copy.41, bf16[1,256,1,256]{1,0,3,2:T(2,128)(2,1)} %collective-permute-done.2), kind=kOutput, calls=%fused_computation.1 | convolution fusion | flops 2416705536 | bytes 4587520 | tf_op jit(solution)/shard_map/conv_general_dilated | solution.py:34
  168.2 0.0 all-reduce.2.cloned.1.call-update
  168.3 0.0 all-to-all-done
  168.3 1.9 copy.47
  170.2 261.3 %all-reduce.2.cloned.1.call-done = f32[3,3,256,128]{3,2,1,0:T(8,128)} async-done(((f32[3,3,256,128]{3,2,1,0:T(8,128)}), f32[3,3,256,128]{3,2,1,0:T(8,128)}) %all-reduce.2.cloned.1.call-update) | async-done | bytes 1179664 | tf_op jit(solution)/shard_map/psum | solution.py:65
  431.5 2.4 copy.49
  (1 shorter events, 0.0 us)
Async XLA Ops:
  7.2 74.3 %copy-start = (bf16[3,3,256,128]{3,2,1,0:T(8,128)(2,1)S(1)}, bf16[3,3,256,128]{3,2,1,0:T(8,128)(2,1)}, u32[]{:S(2)}) copy-start(bf16[3,3,256,128]{3,2,1,0:T(8,128)(2,1)} %param.5) | copy-start | bytes 1769476
  25.6 62.3 %all-to-all-start.1 = ((bf16[1,64,64,256]{3,1,0,2:T(8,128)(2,1)}), bf16[1,64,64,256]{3,1,0,2:T(8,128)(2,1)S(1)}, u32[]{:S(2)}, u32[]{:S(2)}) async-start(bf16[1,64,64,256]{3,1,0,2:T(8,128)(2,1)} %copy.38), calls=%async_computation.1 | async-start | bytes 4194304 | tf_op jit(solution)/shard_map/all_to_all | solution.py:57
  32.9 35.3 %collective-permute-start = (bf16[1,128,1,256]{3,2,1,0:T(2,128)(2,1)S(1)}, bf16[1,128,1,256]{3,2,1,0:T(2,128)(2,1)S(1)}, u32[]{:S(2)}, u32[]{:S(2)}) collective-permute-start(bf16[1,128,1,256]{3,2,1,0:T(2,128)(2,1)S(1)} %get-tuple-element.4), channel_id=1, source_target_pairs={{0,1},{1,2},{2,3},{4,5},{5,6},{6,7},{8,9},{9,10},{10,11},{12,13},{... | collective-permute-start | bytes 196616 | tf_op jit(solution)/shard_map/ppermute | solution.py:15
  36.8 31.4 %collective-permute-start.1 = (bf16[1,128,1,256]{3,2,1,0:T(2,128)(2,1)S(1)}, bf16[1,128,1,256]{3,2,1,0:T(2,128)(2,1)S(1)}, u32[]{:S(2)}, u32[]{:S(2)}) collective-permute-start(bf16[1,128,1,256]{3,2,1,0:T(2,128)(2,1)S(1)} %get-tuple-element.5), channel_id=1, source_target_pairs={{1,0},{2,1},{3,2},{5,4},{6,5},{7,6},{9,8},{10,9},{11,10},{13,12},{... | collective-permute-start | bytes 196616 | tf_op jit(solution)/shard_map/ppermute | solution.py:17
  76.9 4.6 %copy-start.2 = (pred[8,33]{0,1:T(8,128)(4,1)S(1)}, pred[8,33]{0,1:T(8,128)(4,1)}, u32[]{:S(2)}) copy-start(pred[8,33]{0,1:T(8,128)(4,1)} %constant.8) | copy-start | bytes 796
  96.6 40.8 %collective-permute-start.2 = (bf16[1,256,1,256]{1,0,3,2:T(2,128)(2,1)}, bf16[1,256,1,256]{1,0,3,2:T(2,128)(2,1)}, u32[]{:S(2)}, u32[]{:S(2)}) collective-permute-start(bf16[1,256,1,256]{1,0,3,2:T(2,128)(2,1)} %get-tuple-element.2), channel_id=1, source_target_pairs={{0,1},{1,2},{2,3},{4,5},{5,6},{6,7},{8,9},{9,10},{10,11},{12,13},{... | collective-permute-start | bytes 393224 | tf_op jit(solution)/shard_map/ppermute | solution.py:15
  114.1 23.4 %collective-permute-start.3 = (bf16[1,256,1,256]{1,0,3,2:T(2,128)(2,1)S(1)}, bf16[1,256,1,256]{1,0,3,2:T(2,128)(2,1)}, u32[]{:S(2)}, u32[]{:S(2)}) collective-permute-start(bf16[1,256,1,256]{1,0,3,2:T(2,128)(2,1)S(1)} %get-tuple-element.3), channel_id=1, source_target_pairs={{1,0},{2,1},{3,2},{5,4},{6,5},{7,6},{9,8},{10,9},{11,10},{13,12},{... | collective-permute-start | bytes 393224 | tf_op jit(solution)/shard_map/ppermute | solution.py:17
  126.0 11.5 %copy-start.1 = (bf16[1,128,16,256]{1,0,3,2:T(2,128)(2,1)S(1)}, bf16[1,128,16,256]{1,0,3,2:T(2,128)(2,1)}, u32[]{:S(2)}) copy-start(bf16[1,128,16,256]{1,0,3,2:T(2,128)(2,1)} %copy.44) | copy-start | bytes 3145732
  133.2 35.0 %all-to-all-start = ((bf16[1,256,8,128]{3,2,0,1:T(8,128)(2,1)}), bf16[1,256,8,128]{3,2,0,1:T(8,128)(2,1)}, u32[]{:S(2)}, u32[]{:S(2)}) async-start(bf16[1,256,8,128]{3,2,0,1:T(8,128)(2,1)} %copy.34), calls=%async_computation | async-start | bytes 1048576 | tf_op jit(solution)/shard_map/all_to_all | solution.py:62
  137.4 294.1 %all-reduce.2.cloned.1.call-start = ((), (), s32[]{:S(2)}) async-start(), calls=%async_computation.2 | async-start | bytes 2359296 | tf_op jit(solution)/shard_map/psum | solution.py:65
Sparse Core Ops, SparseCore 0:
  168.4 263.0 all-reduce.1
where the time goes:
time: 442 us; the launch traced here: 441 us
  waiting for transfers between devices  287 us (65%)
  local copies, waits for them, and re-layouts  62.3 us (14%)
  starting transfers between devices  34.5 us (8%)
  matrix products  33.8 us (8%)
  between operations  14.2 us (3%)
  other arithmetic  9.27 us (2%)
    psum x1, waiting for transfers between devices, body(): total = lax.psum(partial_kernel, ('dp', 'slab'))  261 us
    conv_general_dilated x1, matrix products, kernel_terms(): lax.conv_general_dilated(padded_up, grad_rows, (1, 1), ((0, 0), (1, 1)),...  30.8 us
    ppermute x2, waiting for transfers between devices, extended(): lax.ppermute(tail, axis, [(i, (i + 1) % count) for i in range(ends)])  25.4 us
    ppermute x2, starting transfers between devices, extended(): lax.ppermute(tail, axis, [(i, (i + 1) % count) for i in range(ends)])  21.4 us
    broadcast_in_dim x4, local copies, waits for them, and re-layouts, upsample(): return jnp.repeat(jnp.repeat(field, 2, axis=2), 2, axis=3)  17.1 us
    conv_general_dilated x5, local copies, waits for them, and re-layouts, input_terms(): lax.conv_general_dilated(padded_grad, flipped, (1, 1), ((0, 0), (1, 1)),...  12.5 us
    unnamed x9, local copies, waits for them, and re-layouts  9.55 us
  transfers between devices with their start and end apart: 7, of which 2 were waited for; matrix products, arithmetic and copies ran while one was open for 17% of the time, Pallas kernels for 0%

commit v1 on v0

--- a/solution.py
+++ b/solution.py
@@ -62,7 +62,7 @@
     returned = lax.all_to_all(
         grad_low.astype(jnp.bfloat16), "slab", split_axis=1, concat_axis=2, tiled=True
     ).astype(grad_low.dtype)
-    total = lax.psum(partial_kernel, ("dp", "slab"))
+    total = lax.psum(lax.psum(partial_kernel, "dp"), "slab")
     return (returned.astype(jnp.bfloat16), total)
 
 

time: 442 us -> 984 us (2.23)
  waiting for transfers between devices: 287 us -> 797 us
  blocking collectives: 0 us -> 73 us
  starting transfers between devices: 34.5 us -> 8.62 us
  local copies, waits for them, and re-layouts: 62.3 us -> 52.1 us
    psum x1 -> x2, waiting for transfers between devices: 261 us -> 789 us  [body(): total = lax.psum(lax.psum(partial_kernel, 'dp'), 'slab')]
    all_to_all x0 -> x2, blocking collectives: none -> 73 us  [the longest x1 53.9 us: body(): lax.all_to_all(upsample(images), 'slab', split_axis=2, concat_axis=1, til...]
    ppermute x2, waiting for transfers between devices: 25.4 us -> 1.2 us  [extended(): lax.ppermute(tail, axis, [(i, (i + 1) % count) for i in range(ends)])]
    ppermute x2, starting transfers between devices: 21.4 us -> 5.77 us  [extended(): lax.ppermute(tail, axis, [(i, (i + 1) % count) for i in range(ends)])]
    all_to_all x2 -> x0, starting transfers between devices: 10.1 us -> none  [the longest x1 5.89 us: body(): lax.all_to_all(upsample(images), 'slab', split_axis=2, concat_axis=1, til...]
  transfers between devices with their start and end apart: 7 -> 6, of which waited for: 2 -> 5; matrix products, arithmetic and copies ran while one was open for 17% -> 3% of each run, Pallas kernels for 0% -> 0%
where the time goes in v1:
time: 984 us; the launch traced here: 983 us
  waiting for transfers between devices  797 us (81%)
  blocking collectives  73 us (7%)
  local copies, waits for them, and re-layouts  52.1 us (5%)
  matrix products  31.5 us (3%)
  between operations  14.2 us (1%)
    psum x2, waiting for transfers between devices, body(): total = lax.psum(lax.psum(partial_kernel, 'dp'), 'slab')  789 us
    all_to_all x1, blocking collectives, body(): lax.all_to_all(upsample(images), 'slab', split_axis=2, concat_axis=1, til...  53.9 us
    conv_general_dilated x1, matrix products, kernel_terms(): lax.conv_general_dilated(padded_up, grad_rows, (1, 1), ((0, 0), (1, 1)),...  28.5 us
  transfers between devices with their start and end apart: 6, of which 5 were waited for; matrix products, arithmetic and copies ran while one was open for 3% of the time, Pallas kernels for 0%

profile of v1, /device:TPU:6, one launch (start us, length us, event | category | flops | bytes accessed | tf_op | source)
XLA Modules:
  0.0 983.0 jit_solution(1813466868000739039)
XLA Ops:
  7.2 0.0 copy-start
  7.2 0.0 all-reduce.3.cloned.1.call-start
  7.2 1.3 copy.36
  8.5 1.3 broadcast_in_dim.10
  9.8 4.7 copy.37
  14.5 3.3 broadcast_in_dim.12
  17.8 7.0 copy.38
  24.8 53.9 %all_to_all.36 = bf16[1,64,64,256]{3,1,0,2:T(8,128)(2,1)S(1)} all-to-all(bf16[1,64,64,256]{3,1,0,2:T(8,128)(2,1)S(1)} %copy.38), channel_id=1, replica_groups=mesh['dp'=64,'slab'=4] {'slab'}, dimensions={2} | all-to-all | bytes 4194304 | tf_op jit(solution)/shard_map/all_to_all | solution.py:57
  78.7 1.2 copy.39
  79.9 0.2 copy.40
  80.1 5.1 copy.41
  85.2 1.6 fusion.13
  86.7 2.1 collective-permute-start.2
  88.9 1.5 collective-permute-start.3
  90.3 4.5 copy.44
  94.8 0.0 collective-permute-done.2
  94.8 2.3 collective-permute-done.3
  97.1 0.0 copy-start.1
  97.1 28.5 %fusion = f32[3,3,256,128]{3,2,1,0:T(8,128)} fusion(bf16[1,128,16,256]{1,0,3,2:T(2,128)(2,1)} %copy.44, bf16[1,256,1,256]{1,0,3,2:T(2,128)(2,1)S(1)} %collective-permute-done.3, bf16[1,256,16,256]{1,0,3,2:T(2,128)(2,1)} %copy.41, bf16[1,256,1,256]{1,0,3,2:T(2,128)(2,1)S(1)} %collective-permute-done.2), kind=kOutput, calls=%fused_computation.1 | convolution fusion | flops 2416705536 | bytes 4587520 | tf_op jit(solution)/shard_map/conv_general_dilated | solution.py:34
  125.6 0.0 all-reduce.3.cloned.1.call-update
  125.6 0.0 all-reduce.5.cloned.1.call-start
  125.7 0.0 copy-done.1
  125.7 0.2 fusion.14
  125.9 3.6 collective-permute-start
  129.5 1.3 collective-permute-start.1
  130.8 1.2 collective-permute-done
  132.0 4.4 collective-permute-done.1
  136.4 1.1 maximum_bitcast_fusion
  137.5 2.0 copy.45
  139.5 1.6 pad.clone
  141.1 0.0 copy-start.2
  141.1 0.4 reshape.29
  141.6 0.2 copy.32
  141.8 0.0 copy-done
  141.8 0.0 copy-done.2
  141.8 3.0 broadcast_select_fusion
  144.8 3.3 copy.33
  148.1 720.5 %all-reduce.3.cloned.1.call-done = f32[3,3,256,128]{3,2,1,0:T(8,128)} async-done(((f32[3,3,256,128]{3,2,1,0:T(8,128)}), f32[3,3,256,128]{3,2,1,0:T(8,128)}) %all-reduce.3.cloned.1.call-update) | async-done | bytes 1179664 | tf_op jit(solution)/shard_map/psum | solution.py:65
  868.7 0.0 all-reduce.5.cloned.1.call-update
  868.7 4.6 slice_bitcast_fusion
  873.3 5.8 reshape.26
  879.1 5.7 reduce_sum.9
  884.9 0.6 copy.34
  885.4 19.1 %all_to_all.37 = bf16[1,256,8,128]{3,2,0,1:T(8,128)(2,1)S(1)} all-to-all(bf16[1,256,8,128]{3,2,0,1:T(8,128)(2,1)S(1)} %copy.34), channel_id=1, replica_groups=mesh['dp'=64,'slab'=4] {'slab'}, dimensions={1} | all-to-all | bytes 1048576 | tf_op jit(solution)/shard_map/all_to_all | solution.py:62
  904.5 0.9 copy.47
  905.4 68.4 %all-reduce.5.cloned.1.call-done = f32[3,3,256,128]{3,2,1,0:T(8,128)} async-done(((f32[3,3,256,128]{3,2,1,0:T(8,128)}), f32[3,3,256,128]{3,2,1,0:T(8,128)}) %all-reduce.5.cloned.1.call-update) | async-done | bytes 1179664 | tf_op jit(solution)/shard_map/psum | solution.py:65
  973.8 2.4 copy.50
  (1 shorter events, 0.0 us)
Async XLA Ops:
  7.2 134.6 %copy-start = (bf16[3,3,256,128]{3,2,1,0:T(8,128)(2,1)S(1)}, bf16[3,3,256,128]{3,2,1,0:T(8,128)(2,1)}, u32[]{:S(2)}) copy-start(bf16[3,3,256,128]{3,2,1,0:T(8,128)(2,1)} %param.5) | copy-start | bytes 1769476
  7.2 861.5 %all-reduce.3.cloned.1.call-start = ((), (), s32[]{:S(2)}) async-start(), calls=%async_computation.2 | async-start | bytes 2359296 | tf_op jit(solution)/shard_map/psum | solution.py:65
  86.7 8.1 collective-permute-start.2
  88.9 8.3 collective-permute-start.3
  97.1 28.5 %copy-start.1 = (bf16[1,128,16,256]{3,2,1,0:T(8,128)(2,1)S(1)}, bf16[1,128,16,256]{3,2,1,0:T(8,128)(2,1)}, u32[]{:S(2)}) copy-start(bf16[1,128,16,256]{3,2,1,0:T(8,128)(2,1)} %param.4) | copy-start | bytes 3145732
  125.6 848.2 %all-reduce.5.cloned.1.call-start = ((), (), s32[]{:S(2)}) async-start(), calls=%async_computation.3 | async-start | bytes 2359296 | tf_op jit(solution)/shard_map/psum | solution.py:65
  125.9 6.1 collective-permute-start
  129.5 6.9 collective-permute-start.1
  141.1 0.7 copy-start.2
Sparse Core Ops, SparseCore 0:
  125.7 742.8 all-reduce.2
  871.3 102.3 all-reduce.4
